TPU v7x, 32 devices: a whole 2x2x4 slice. The times are simulated.
32 devices in a mesh: dp: 2 (over x), row: 4 (over z), col: 4 (over y, core).
Axes of the slice: x: 2, y: 2, z: 4, core: 2. Of those that a mesh axis runs over, the one named last changes fastest.
Arguments:
- layer_input: bfloat16 [1536, 6144], P(('dp', 'col'), 'row'), may hold values from -125 to 125
- grad_output: bfloat16 [1536, 6144], P(('dp', 'col'), 'row'), may hold values from -6 to 6
- pre_activation: bfloat16 [1536, 24576], P(('dp', 'row'), 'col'), may hold values from -6 to 6
- norm_gain_vector: float32 [6144], P('row'), may hold values from 0.5 to 1.5
- up_weight: bfloat16 [6144, 24576], P('row', 'col'), may hold values from -0.078125 to 0.078125
- down_weight: bfloat16 [24576, 6144], P('col', 'row'), may hold values from -0.0390625 to 0.0390625
Outputs:
- input_gradient: float32 [1536, 6144], P(('dp', 'col'), 'row')
- grad_up: float32 [6144, 24576], P(('row', 'dp'), 'col')
- grad_down: float32 [24576, 6144], P('col', ('row', 'dp'))
- grad_bias: float32 [24576], P('col')
- gain_gradient: float32 [6144], P('row')
All inputs are finite; a program needn't handle non-finite values.
Results may differ from a plain program's by a relative error of at most 0.0055.
Values may be sent and summed in bfloat16 or wider, within the bound.
A program may use at most 256 MiB of HBM per device.

v0:
```python
import jax
import jax.numpy as jnp
from jax import lax
from jax.sharding import PartitionSpec as P

CHUNKS = 4
epsilon = 1e-06


def gelu_parts(pre_float):
    normal_cdf = 0.5 * (1.0 + lax.erf(pre_float * 0.7071067811865476))
    normal_pdf = jnp.exp(-0.5 * pre_float * pre_float) * 0.3989422804014327
    return (pre_float * normal_cdf, normal_cdf + pre_float * normal_pdf)


def contract_last(left, right):
    return lax.dot_general(
        left, right, (((1,), (1,)), ((), ())), preferred_element_type=jnp.float32
    )


def contract_first(left, right):
    return lax.dot_general(
        left, right, (((0,), (0,)), ((), ())), preferred_element_type=jnp.float32
    )


def build(sizes):
    swap = [(0, 1), (1, 0)]
    two = sizes["dp"] == 2

    def per_device(
        layer_input, grad_output, pre_activation, norm_gain_vector, up_weight, down_weight
    ):
        model_width = layer_input.shape[1] * sizes["row"]
        hidden = pre_activation.shape[1]
        chunks = CHUNKS if hidden % (CHUNKS * 128) == 0 else 1
        step = hidden // chunks
        me = lax.axis_index("dp")
        grad_all = lax.all_gather(grad_output, "col", axis=0, tiled=True)
        x = layer_input.astype(jnp.float32)
        sum_rows, square_rows = lax.psum((jnp.sum(x, axis=1), jnp.sum(x * x, axis=1)), "row")
        mean = sum_rows / model_width
        inv_std = 1.0 / jnp.sqrt(square_rows / model_width - mean * mean + epsilon)
        xhat = (x - mean[:, None]) * inv_std[:, None]
        normed = (xhat * norm_gain_vector[None, :]).astype(jnp.bfloat16)
        normed_all = lax.all_gather(normed, "col", axis=0, tiled=True)
        half = layer_input.shape[1] // sizes["dp"]

        def part(array, index):
            return lax.dynamic_slice_in_dim(array, index * half, half, axis=1)

        if two:
            normed_mine, normed_other = (part(normed_all, me), part(normed_all, 1 - me))
            grad_mine, grad_other = (part(grad_all, me), part(grad_all, 1 - me))

        def up_of(hid):
            if not two:
                return lax.psum_scatter(
                    contract_first(normed_all, hid), "dp", scatter_dimension=0, tiled=True
                )
            away = contract_first(normed_other, hid).astype(jnp.bfloat16)
            got = lax.ppermute(away, "dp", swap)
            return contract_first(normed_mine, hid) + got.astype(jnp.float32)

        def down_of(act):
            if not two:
                return lax.psum_scatter(
                    contract_first(act, grad_all), "dp", scatter_dimension=1, tiled=True
                )
            away = contract_first(act, grad_other).astype(jnp.bfloat16)
            got = lax.ppermute(away, "dp", swap)
            return contract_first(act, grad_mine) + got.astype(jnp.float32)

        ups, downs, biases, total = ([], [], [], None)
        for k in range(chunks):
            cut = slice(k * step, (k + 1) * step)
            value, slope = gelu_parts(pre_activation[:, cut].astype(jnp.float32))
            grad_act = lax.psum_scatter(
                contract_last(grad_all, down_weight[cut]).astype(jnp.bfloat16),
                "row",
                scatter_dimension=0,
                tiled=True,
            )
            act_all = lax.all_gather(value.astype(jnp.bfloat16), "row", axis=0, tiled=True)
            grad_hidden = (grad_act.astype(jnp.float32) * slope).astype(jnp.bfloat16)
            hid_all = lax.all_gather(grad_hidden, "row", axis=0, tiled=True)
            downs.append(down_of(act_all))
            ups.append(up_of(hid_all))
            biases.append(jnp.sum(hid_all.astype(jnp.float32), axis=0))
            term = contract_last(hid_all, up_weight[:, cut])
            total = term if total is None else total + term
        bias = jnp.concatenate(biases)
        grad_bias = bias + lax.ppermute(bias, "dp", swap) if two else lax.psum(bias, "dp")
        grad_up = jnp.concatenate(ups, axis=1)
        grad_down = jnp.concatenate(downs, axis=0)
        grad_normed = lax.psum_scatter(
            total.astype(jnp.bfloat16), "col", scatter_dimension=0, tiled=True
        ).astype(jnp.float32)
        scaled = grad_normed * norm_gain_vector[None, :]
        first, second = lax.psum((jnp.sum(scaled, axis=1), jnp.sum(scaled * xhat, axis=1)), "row")
        input_gradient = inv_std[:, None] * (
            scaled - first[:, None] / model_width - xhat * (second[:, None] / model_width)
        )
        gain_gradient = lax.psum(jnp.sum(grad_normed * xhat, axis=0), ("dp", "col"))
        return (input_gradient, grad_up, grad_down, grad_bias, gain_gradient)

    return per_device


def solution(mesh):
    placed = (
        P(("dp", "col"), "row"),
        P(("dp", "col"), "row"),
        P(("dp", "row"), "col"),
        P("row"),
        P("row", "col"),
        P("col", "row"),
    )
    return jax.shard_map(
        build(dict(mesh.shape)),
        mesh=mesh,
        in_specs=placed,
        out_specs=(
            P(("dp", "col"), "row"),
            P(("row", "dp"), "col"),
            P("col", ("row", "dp")),
            P("col"),
            P("row"),
        ),
        check_vma=False,
    )
```

profile of v0, /device:TPU:0, one launch (start us, length us, event | category | flops | bytes accessed | tf_op | source)
XLA Modules:
  0.0 974.1 jit_solution(11959575978303377760)
XLA Ops:
  7.9 28.4 %all-gather.11.cloned.1.call-done = bf16[768,1536]{1,0:T(8,128)(2,1)} async-done(((bf16[192,1536]{1,0:T(8,128)(2,1)}), bf16[768,1536]{1,0:T(8,128)(2,1)}) %all-gather.11.cloned.1.call-update) | async-done | bytes 2359312 | tf_op jit(solution)/shard_map/all_gather | solution.py:40
  36.3 8.3 fusion.22
  68.8 23.7 %reduce-scatter.10.cloned.1.call-done = bf16[192,1536]{1,0:T(8,128)(2,1)} async-done(((bf16[768,1536]{1,0:T(8,128)(2,1)}), bf16[192,1536]{1,0:T(8,128)(2,1)}) %reduce-scatter.10.cloned.1.call-update) | async-done | bytes 589840 | tf_op jit(solution)/shard_map/reduce_scatter | solution.py:79
  92.5 50.0 %reduce-scatter.12.cloned.1.call-done = bf16[192,1536]{1,0:T(8,128)(2,1)} async-done(((bf16[768,1536]{1,0:T(8,128)(2,1)}), bf16[192,1536]{1,0:T(8,128)(2,1)}) %reduce-scatter.12.cloned.1.call-update) | async-done | bytes 589840 | tf_op jit(solution)/shard_map/reduce_scatter | solution.py:79
  142.5 49.3 %reduce-scatter.6.cloned.1.call-done = bf16[192,1536]{1,0:T(8,128)(2,1)} async-done(((bf16[768,1536]{1,0:T(8,128)(2,1)}), bf16[192,1536]{1,0:T(8,128)(2,1)}) %reduce-scatter.6.cloned.1.call-update) | async-done | bytes 589840 | tf_op jit(solution)/shard_map/reduce_scatter | solution.py:79
  191.8 49.3 %reduce-scatter.8.cloned.1.call-done = bf16[192,1536]{1,0:T(8,128)(2,1)} async-done(((bf16[768,1536]{1,0:T(8,128)(2,1)}), bf16[192,1536]{1,0:T(8,128)(2,1)}) %reduce-scatter.8.cloned.1.call-update) | async-done | bytes 589840 | tf_op jit(solution)/shard_map/reduce_scatter | solution.py:79
  251.9 44.4 %all-gather.13.cloned.1.call-done = bf16[768,1536]{1,0:T(8,128)(2,1)} async-done(((bf16[192,1536]{1,0:T(8,128)(2,1)}), bf16[768,1536]{1,0:T(8,128)(2,1)}) %all-gather.13.cloned.1.call-update) | async-done | bytes 2359312 | tf_op jit(solution)/shard_map/all_gather | solution.py:87
  296.3 9.1 fusion.12
  305.4 41.8 %all-gather.17.cloned.1.call-done = bf16[768,1536]{1,0:T(8,128)(2,1)} async-done(((bf16[192,1536]{1,0:T(8,128)(2,1)}), bf16[768,1536]{1,0:T(8,128)(2,1)}) %all-gather.17.cloned.1.call-update) | async-done | bytes 2359312 | tf_op jit(solution)/shard_map/all_gather | solution.py:87
  347.3 9.1 fusion.4
  356.3 41.3 %all-gather.15.cloned.1.call-done = bf16[768,1536]{1,0:T(8,128)(2,1)} async-done(((bf16[192,1536]{1,0:T(8,128)(2,1)}), bf16[768,1536]{1,0:T(8,128)(2,1)}) %all-gather.15.cloned.1.call-update) | async-done | bytes 2359312 | tf_op jit(solution)/shard_map/all_gather | solution.py:87
  397.6 9.0 fusion.8
  406.6 41.3 %all-gather.19.cloned.1.call-done = bf16[768,1536]{1,0:T(8,128)(2,1)} async-done(((bf16[192,1536]{1,0:T(8,128)(2,1)}), bf16[768,1536]{1,0:T(8,128)(2,1)}) %all-gather.19.cloned.1.call-update) | async-done | bytes 2359312 | tf_op jit(solution)/shard_map/all_gather | solution.py:87
  447.9 12.6 %add_convert_fusion = bf16[768,1536]{1,0:T(8,128)(2,1)} fusion(f32[768,1536]{1,0:T(8,128)} %fusion.4, f32[768,1536]{1,0:T(8,128)} %fusion.12, f32[768,1536]{1,0:T(8,128)} %fusion.8, bf16[768,1536]{1,0:T(8,128)(2,1)} %all-gather.19.cloned.1.call-done, bf16[1536,6144]{1,0:T(8,128)(2,1)} %param.10), kind=kOutput, calls=%fused_computation.14 | convolution fusion | flops 3628597248 | bytes 23592960 | tf_op jit(solution)/shard_map/dot_general | solution.py:17
  461.9 10.4 %all-reduce.1 = (f32[192]{0:T(256)S(1)}, f32[192]{0:T(256)S(1)}) all-reduce(f32[192]{0:T(256)S(1)} %get-tuple-element.9, f32[192]{0:T(256)S(1)} %get-tuple-element.8), channel_id=1, replica_groups=mesh['dp'=2,'row'=4,'col'=4] {'row'}, use_global_device_ids=true, to_apply=%region_3.0 | all-reduce | flops 384 | bytes 3072 | tf_op jit(solution)/shard_map/psum | solution.py:42
  472.3 26.1 %all-gather.29.cloned.1.call-done = bf16[768,1536]{1,0:T(8,128)(2,1)} async-done(((bf16[192,1536]{1,0:T(8,128)(2,1)}), bf16[768,1536]{1,0:T(8,128)(2,1)}) %all-gather.29.cloned.1.call-update) | async-done | bytes 2359312 | tf_op jit(solution)/shard_map/all_gather | solution.py:85
  505.0 43.8 %all-gather.27.cloned.1.call-done = bf16[768,1536]{1,0:T(8,128)(2,1)} async-done(((bf16[192,1536]{1,0:T(8,128)(2,1)}), bf16[768,1536]{1,0:T(8,128)(2,1)}) %all-gather.27.cloned.1.call-update) | async-done | bytes 2359312 | tf_op jit(solution)/shard_map/all_gather | solution.py:85
  555.3 43.6 %all-gather.25.cloned.1.call-done = bf16[768,1536]{1,0:T(8,128)(2,1)} async-done(((bf16[192,1536]{1,0:T(8,128)(2,1)}), bf16[768,1536]{1,0:T(8,128)(2,1)}) %all-gather.25.cloned.1.call-update) | async-done | bytes 2359312 | tf_op jit(solution)/shard_map/all_gather | solution.py:85
  605.6 44.3 %all-gather.23.cloned.1.call-done = bf16[768,1536]{1,0:T(8,128)(2,1)} async-done(((bf16[192,1536]{1,0:T(8,128)(2,1)}), bf16[768,1536]{1,0:T(8,128)(2,1)}) %all-gather.23.cloned.1.call-update) | async-done | bytes 2359312 | tf_op jit(solution)/shard_map/all_gather | solution.py:85
  656.4 27.5 %reduce-scatter.14.cloned.1.call-done = bf16[192,1536]{1,0:T(8,128)(2,1)} async-done(((bf16[768,1536]{1,0:T(8,128)(2,1)}), bf16[192,1536]{1,0:T(8,128)(2,1)}) %reduce-scatter.14.cloned.1.call-update) | async-done | bytes 589840 | tf_op jit(solution)/shard_map/reduce_scatter | solution.py:97
  692.3 16.4 %collective-permute-done.8 = f32[6144]{0:T(1024)S(1)} collective-permute-done((f32[6144]{0:T(1024)S(1)}, f32[6144]{0:T(1024)S(1)}, u32[]{:S(2)}, u32[]{:S(2)}) %collective-permute-start.8) | collective-permute-done | bytes 24608 | tf_op jit(solution)/shard_map/ppermute | solution.py:94
  758.1 9.7 all-reduce
  767.8 135.6 %psum.39 = f32[1536]{0:T(1024)} all-reduce(f32[1536]{0:T(1024)S(1)} %get-tuple-element.5), channel_id=1, replica_groups=mesh['dp'=2,'row'=4,'col'=4] {'dp','col'}, use_global_device_ids=true, to_apply=%region_18.0 | all-reduce | flops 1536 | bytes 12288 | tf_op jit(solution)/shard_map/psum | solution.py:105
  921.5 36.5 %collective-permute-done.3 = bf16[768,1536]{1,0:T(8,128)(2,1)S(1)} collective-permute-done((bf16[768,1536]{1,0:T(8,128)(2,1)S(1)}, bf16[768,1536]{1,0:T(8,128)(2,1)S(1)}, u32[]{:S(2)}, u32[]{:S(2)}) %collective-permute-start.3) | collective-permute-done | bytes 2359328 | tf_op jit(solution)/shard_map/ppermute | solution.py:63
  (138 shorter events, 148.1 us)
Async XLA Ops:
  7.2 29.2 %all-gather.11.cloned.1.call-start = ((), (), s32[]{:S(2)}) async-start(), calls=%async_computation.5 | async-start | bytes 2949120 | tf_op jit(solution)/shard_map/all_gather | solution.py:40
  7.9 84.6 %reduce-scatter.10.cloned.1.call-start = ((), (), s32[]{:S(2)}) async-start(), calls=%async_computation.10 | async-start | bytes 2949120 | tf_op jit(solution)/shard_map/reduce_scatter | solution.py:79
  44.7 97.9 %reduce-scatter.12.cloned.1.call-start = ((), (), s32[]{:S(2)}) async-start(), calls=%async_computation.12 | async-start | bytes 2949120 | tf_op jit(solution)/shard_map/reduce_scatter | solution.py:79
  53.7 138.1 %reduce-scatter.6.cloned.1.call-start = ((), (), s32[]{:S(2)}) async-start(), calls=%async_computation.6 | async-start | bytes 2949120 | tf_op jit(solution)/shard_map/reduce_scatter | solution.py:79
  61.3 179.8 %reduce-scatter.8.cloned.1.call-start = ((), (), s32[]{:S(2)}) async-start(), calls=%async_computation.8 | async-start | bytes 2949120 | tf_op jit(solution)/shard_map/reduce_scatter | solution.py:79
  68.8 227.6 %all-gather.13.cloned.1.call-start = ((), (), s32[]{:S(2)}) async-start(), calls=%async_computation.7 | async-start | bytes 2949120 | tf_op jit(solution)/shard_map/all_gather | solution.py:87
  246.8 100.4 %all-gather.17.cloned.1.call-start = ((), (), s32[]{:S(2)}) async-start(), calls=%async_computation.11 | async-start | bytes 2949120 | tf_op jit(solution)/shard_map/all_gather | solution.py:87
  247.6 150.0 %all-gather.15.cloned.1.call-start = ((), (), s32[]{:S(2)}) async-start(), calls=%async_computation.9 | async-start | bytes 2949120 | tf_op jit(solution)/shard_map/all_gather | solution.py:87
  248.3 199.6 %all-gather.19.cloned.1.call-start = ((), (), s32[]{:S(2)}) async-start(), calls=%async_computation.13 | async-start | bytes 2949120 | tf_op jit(solution)/shard_map/all_gather | solution.py:87
  249.1 249.3 %all-gather.29.cloned.1.call-start = ((), (), s32[]{:S(2)}) async-start(), calls=%async_computation.19 | async-start | bytes 2949120 | tf_op jit(solution)/shard_map/all_gather | solution.py:85
  249.6 299.1 %all-gather.27.cloned.1.call-start = ((), (), s32[]{:S(2)}) async-start(), calls=%async_computation.18 | async-start | bytes 2949120 | tf_op jit(solution)/shard_map/all_gather | solution.py:85
  250.4 348.6 %all-gather.25.cloned.1.call-start = ((), (), s32[]{:S(2)}) async-start(), calls=%async_computation.17 | async-start | bytes 2949120 | tf_op jit(solution)/shard_map/all_gather | solution.py:85
  251.0 398.9 %all-gather.23.cloned.1.call-start = ((), (), s32[]{:S(2)}) async-start(), calls=%async_computation.16 | async-start | bytes 2949120 | tf_op jit(solution)/shard_map/all_gather | solution.py:85
  251.7 432.2 %reduce-scatter.14.cloned.1.call-start = ((), (), s32[]{:S(2)}) async-start(), calls=%async_computation.14 | async-start | bytes 2949120 | tf_op jit(solution)/shard_map/reduce_scatter | solution.py:97
  460.6 274.4 %all-gather.21.cloned.1.call-start = ((), (), s32[]{:S(2)}) async-start(), calls=%async_computation.15 | async-start | bytes 2949120 | tf_op jit(solution)/shard_map/all_gather | solution.py:47
  503.5 205.9 %collective-permute-start.7 = (bf16[1536,768]{1,0:T(8,128)(2,1)}, bf16[1536,768]{1,0:T(8,128)(2,1)}, u32[]{:S(2)}, u32[]{:S(2)}) collective-permute-start(bf16[1536,768]{1,0:T(8,128)(2,1)} %convolution_convert_fusion), channel_id=1, source_target_pairs={{0,16},{16,0},{1,17},{17,1},{2,18},{18,2},{3,19},{19,3},{4,20},{20... | collective-permute-start | bytes 7077896 | tf_op jit(solution)/shard_map/ppermute | solution.py:72
  553.9 163.1 %collective-permute-start.6 = (bf16[1536,768]{1,0:T(8,128)(2,1)}, bf16[1536,768]{1,0:T(8,128)(2,1)}, u32[]{:S(2)}, u32[]{:S(2)}) collective-permute-start(bf16[1536,768]{1,0:T(8,128)(2,1)} %convolution_convert_fusion.1), channel_id=1, source_target_pairs={{0,16},{16,0},{1,17},{17,1},{2,18},{18,2},{3,19},{19,3},{4,20},{20... | collective-permute-start | bytes 7077896 | tf_op jit(solution)/shard_map/ppermute | solution.py:72
  604.1 118.9 %collective-permute-start.5 = (bf16[1536,768]{1,0:T(8,128)(2,1)}, bf16[1536,768]{1,0:T(8,128)(2,1)}, u32[]{:S(2)}, u32[]{:S(2)}) collective-permute-start(bf16[1536,768]{1,0:T(8,128)(2,1)} %convolution_convert_fusion.2), channel_id=1, source_target_pairs={{0,16},{16,0},{1,17},{17,1},{2,18},{18,2},{3,19},{19,3},{4,20},{20... | collective-permute-start | bytes 7077896 | tf_op jit(solution)/shard_map/ppermute | solution.py:72
  655.0 74.1 %collective-permute-start.4 = (bf16[1536,768]{1,0:T(8,128)(2,1)}, bf16[1536,768]{1,0:T(8,128)(2,1)}, u32[]{:S(2)}, u32[]{:S(2)}) collective-permute-start(bf16[1536,768]{1,0:T(8,128)(2,1)} %convolution_convert_fusion.3), channel_id=1, source_target_pairs={{0,16},{16,0},{1,17},{17,1},{2,18},{18,2},{3,19},{19,3},{4,20},{20... | collective-permute-start | bytes 7077896 | tf_op jit(solution)/shard_map/ppermute | solution.py:72
  690.8 18.0 %collective-permute-start.8 = (f32[6144]{0:T(1024)S(1)}, f32[6144]{0:T(1024)S(1)}, u32[]{:S(2)}, u32[]{:S(2)}) collective-permute-start(f32[6144]{0:T(1024)S(1)} %pad_maximum_fusion.2), channel_id=1, source_target_pairs={{0,16},{16,0},{1,17},{17,1},{2,18},{18,2},{3,19},{19,3},{4,20},{20... | collective-permute-start | bytes 73736 | tf_op jit(solution)/shard_map/ppermute | solution.py:94
  740.5 169.2 %collective-permute-start = (bf16[768,1536]{1,0:T(8,128)(2,1)}, bf16[768,1536]{1,0:T(8,128)(2,1)}, u32[]{:S(2)}, u32[]{:S(2)}) collective-permute-start(bf16[768,1536]{1,0:T(8,128)(2,1)} %convolution_convert_fusion.7), channel_id=1, source_target_pairs={{0,16},{16,0},{1,17},{17,1},{2,18},{18,2},{3,19},{19,3},{4,20},{20... | collective-permute-start | bytes 7077896 | tf_op jit(solution)/shard_map/ppermute | solution.py:63
  745.5 168.1 %collective-permute-start.1 = (bf16[768,1536]{1,0:T(8,128)(2,1)}, bf16[768,1536]{1,0:T(8,128)(2,1)}, u32[]{:S(2)}, u32[]{:S(2)}) collective-permute-start(bf16[768,1536]{1,0:T(8,128)(2,1)} %convolution_convert_fusion.6), channel_id=1, source_target_pairs={{0,16},{16,0},{1,17},{17,1},{2,18},{18,2},{3,19},{19,3},{4,20},{20... | collective-permute-start | bytes 7077896 | tf_op jit(solution)/shard_map/ppermute | solution.py:63
  749.5 168.0 %collective-permute-start.2 = (bf16[768,1536]{1,0:T(8,128)(2,1)}, bf16[768,1536]{1,0:T(8,128)(2,1)}, u32[]{:S(2)}, u32[]{:S(2)}) collective-permute-start(bf16[768,1536]{1,0:T(8,128)(2,1)} %convolution_convert_fusion.5), channel_id=1, source_target_pairs={{0,16},{16,0},{1,17},{17,1},{2,18},{18,2},{3,19},{19,3},{4,20},{20... | collective-permute-start | bytes 7077896 | tf_op jit(solution)/shard_map/ppermute | solution.py:63
  907.6 50.4 %collective-permute-start.3 = (bf16[768,1536]{1,0:T(8,128)(2,1)S(1)}, bf16[768,1536]{1,0:T(8,128)(2,1)S(1)}, u32[]{:S(2)}, u32[]{:S(2)}) collective-permute-start(bf16[768,1536]{1,0:T(8,128)(2,1)S(1)} %convolution_convert_fusion.4), channel_id=1, source_target_pairs={{0,16},{16,0},{1,17},{17,1},{2,18},{18,2},{3,19},{19,3},{4,20},{20... | collective-permute-start | bytes 7077896 | tf_op jit(solution)/shard_map/ppermute | solution.py:63
  (27 other events, 472.6 us)
Sparse Core Ops, SparseCore 0:
  9.5 26.7 all-gather.10
  44.8 47.6 reduce-scatter.9
  95.4 47.0 reduce-scatter.11
  144.7 47.0 reduce-scatter.5
  194.0 47.0 reduce-scatter.7
  246.9 49.3 all-gather.12
  298.5 48.7 all-gather.16
  348.8 48.7 all-gather.14
  399.2 48.7 all-gather.18
  449.4 48.9 all-gather.28
  500.0 48.7 all-gather.26
  550.2 48.7 all-gather.24
  601.1 48.7 all-gather.22
  652.3 31.5 reduce-scatter.13
  686.6 24.0 all-gather.20
where the time goes:
time: 981 us; the launch traced here: 974 us
  waiting for transfers between devices  613 us (62%)
  blocking collectives  156 us (16%)
  matrix products  147 us (15%)
  other arithmetic  28.1 us (3%)
  between operations  14.4 us (1%)
  starting transfers between devices  12.4 us (1%)
    reduce_scatter x4, waiting for transfers between devices, per_device(): lax.psum_scatter(contract_last(grad_all, down_weight[cut]).astype(jnp.bfl...  172 us
    all_gather x4, waiting for transfers between devices, per_device(): hid_all = lax.all_gather(grad_hidden, 'row', axis=0, tiled=True)  169 us
    all_gather x4, waiting for transfers between devices, per_device(): lax.all_gather(value.astype(jnp.bfloat16), 'row', axis=0, tiled=True)  158 us
    psum x1, blocking collectives, per_device(): gain_gradient = lax.psum(jnp.sum(grad_normed * xhat, axis=0), ('dp', 'col'))  136 us
    dot_general x16, matrix products, contract_first(): lax.dot_general(left, right, (((0,), (0,)), ((), ())), preferred_element_...  76.5 us
    dot_general x8, matrix products, contract_last(): lax.dot_general(left, right, (((1,), (1,)), ((), ())), preferred_element_...  70.4 us
    ppermute x4, waiting for transfers between devices, up_of(): got = lax.ppermute(away, 'dp', swap)  36.6 us
    all_gather x1, waiting for transfers between devices, per_device(): grad_all = lax.all_gather(grad_output, 'col', axis=0, tiled=True)  28.4 us
  transfers between devices with their start and end apart: 24, of which 16 were waited for; matrix products, arithmetic and copies ran while one was open for 15% of the time, Pallas kernels for 0%

commit v1 on v0

--- a/solution.py
+++ b/solution.py
@@ -102,7 +102,9 @@
         input_gradient = inv_std[:, None] * (
             scaled - first[:, None] / model_width - xhat * (second[:, None] / model_width)
         )
-        gain_gradient = lax.psum(jnp.sum(grad_normed * xhat, axis=0), ("dp", "col"))
+        gain_gradient = jnp.sum(
+            lax.all_gather(jnp.sum(grad_normed * xhat, axis=0), ("dp", "col")), axis=0
+        )
         return (input_gradient, grad_up, grad_down, grad_bias, gain_gradient)
 
     return per_device

time: 981 us -> 988 us (level)
    all_gather x0 -> x1, blocking collectives: none -> 138 us  [per_device(): lax.all_gather(jnp.sum(grad_normed * xhat, axis=0), ('dp', 'col'))]
    psum x1 -> x0, blocking collectives: 136 us -> none  [per_device(): gain_gradient = lax.psum(jnp.sum(grad_normed * xhat, axis=0), ('dp', 'col'))]
where the time goes in v1:
time: 988 us; the launch traced here: 981 us
  waiting for transfers between devices  613 us (62%)
  blocking collectives  159 us (16%)
  matrix products  149 us (15%)
  other arithmetic  28.9 us (3%)
  between operations  14.4 us (1%)
  starting transfers between devices  13.1 us (1%)
    reduce_scatter x4, waiting for transfers between devices, per_device(): lax.psum_scatter(contract_last(grad_all, down_weight[cut]).astype(jnp.bfl...  172 us
    all_gather x4, waiting for transfers between devices, per_device(): hid_all = lax.all_gather(grad_hidden, 'row', axis=0, tiled=True)  169 us
    all_gather x4, waiting for transfers between devices, per_device(): lax.all_gather(value.astype(jnp.bfloat16), 'row', axis=0, tiled=True)  158 us
    all_gather x1, blocking collectives, per_device(): lax.all_gather(jnp.sum(grad_normed * xhat, axis=0), ('dp', 'col'))  138 us
    dot_general x16, matrix products, contract_first(): lax.dot_general(left, right, (((0,), (0,)), ((), ())), preferred_element_...  78.7 us
    dot_general x8, matrix products, contract_last(): lax.dot_general(left, right, (((1,), (1,)), ((), ())), preferred_element_...  70.3 us
    ppermute x4, waiting for transfers between devices, up_of(): got = lax.ppermute(away, 'dp', swap)  36.8 us
    all_gather x1, waiting for transfers between devices, per_device(): grad_all = lax.all_gather(grad_output, 'col', axis=0, tiled=True)  28.4 us
  transfers between devices with their start and end apart: 24, of which 16 were waited for; matrix products, arithmetic and copies ran while one was open for 15% of the time, Pallas kernels for 0%

profile of v1, /device:TPU:0, one launch (start us, length us, event | category | flops | bytes accessed | tf_op | source)
XLA Modules:
  0.0 981.1 jit_solution(17479378747184636288)
XLA Ops:
  7.9 28.4 %all-gather.13.cloned.1.call-done = bf16[768,1536]{1,0:T(8,128)(2,1)} async-done(((bf16[192,1536]{1,0:T(8,128)(2,1)}), bf16[768,1536]{1,0:T(8,128)(2,1)}) %all-gather.13.cloned.1.call-update) | async-done | bytes 2359312 | tf_op jit(solution)/shard_map/all_gather | solution.py:40
  36.3 8.3 fusion.22
  68.8 23.8 %reduce-scatter.10.cloned.1.call-done = bf16[192,1536]{1,0:T(8,128)(2,1)} async-done(((bf16[768,1536]{1,0:T(8,128)(2,1)}), bf16[192,1536]{1,0:T(8,128)(2,1)}) %reduce-scatter.10.cloned.1.call-update) | async-done | bytes 589840 | tf_op jit(solution)/shard_map/reduce_scatter | solution.py:79
  92.5 50.0 %reduce-scatter.12.cloned.1.call-done = bf16[192,1536]{1,0:T(8,128)(2,1)} async-done(((bf16[768,1536]{1,0:T(8,128)(2,1)}), bf16[192,1536]{1,0:T(8,128)(2,1)}) %reduce-scatter.12.cloned.1.call-update) | async-done | bytes 589840 | tf_op jit(solution)/shard_map/reduce_scatter | solution.py:79
  142.5 49.3 %reduce-scatter.6.cloned.1.call-done = bf16[192,1536]{1,0:T(8,128)(2,1)} async-done(((bf16[768,1536]{1,0:T(8,128)(2,1)}), bf16[192,1536]{1,0:T(8,128)(2,1)}) %reduce-scatter.6.cloned.1.call-update) | async-done | bytes 589840 | tf_op jit(solution)/shard_map/reduce_scatter | solution.py:79
  191.8 49.2 %reduce-scatter.8.cloned.1.call-done = bf16[192,1536]{1,0:T(8,128)(2,1)} async-done(((bf16[768,1536]{1,0:T(8,128)(2,1)}), bf16[192,1536]{1,0:T(8,128)(2,1)}) %reduce-scatter.8.cloned.1.call-update) | async-done | bytes 589840 | tf_op jit(solution)/shard_map/reduce_scatter | solution.py:79
  251.9 44.4 %all-gather.15.cloned.1.call-done = bf16[768,1536]{1,0:T(8,128)(2,1)} async-done(((bf16[192,1536]{1,0:T(8,128)(2,1)}), bf16[768,1536]{1,0:T(8,128)(2,1)}) %all-gather.15.cloned.1.call-update) | async-done | bytes 2359312 | tf_op jit(solution)/shard_map/all_gather | solution.py:87
  296.3 9.1 fusion.12
  305.4 41.8 %all-gather.19.cloned.1.call-done = bf16[768,1536]{1,0:T(8,128)(2,1)} async-done(((bf16[192,1536]{1,0:T(8,128)(2,1)}), bf16[768,1536]{1,0:T(8,128)(2,1)}) %all-gather.19.cloned.1.call-update) | async-done | bytes 2359312 | tf_op jit(solution)/shard_map/all_gather | solution.py:87
  347.2 9.1 fusion.4
  356.3 41.3 %all-gather.17.cloned.1.call-done = bf16[768,1536]{1,0:T(8,128)(2,1)} async-done(((bf16[192,1536]{1,0:T(8,128)(2,1)}), bf16[768,1536]{1,0:T(8,128)(2,1)}) %all-gather.17.cloned.1.call-update) | async-done | bytes 2359312 | tf_op jit(solution)/shard_map/all_gather | solution.py:87
  397.6 9.0 fusion.8
  406.6 41.3 %all-gather.21.cloned.1.call-done = bf16[768,1536]{1,0:T(8,128)(2,1)} async-done(((bf16[192,1536]{1,0:T(8,128)(2,1)}), bf16[768,1536]{1,0:T(8,128)(2,1)}) %all-gather.21.cloned.1.call-update) | async-done | bytes 2359312 | tf_op jit(solution)/shard_map/all_gather | solution.py:87
  447.9 12.6 %add_convert_fusion = bf16[768,1536]{1,0:T(8,128)(2,1)} fusion(f32[768,1536]{1,0:T(8,128)} %fusion.4, f32[768,1536]{1,0:T(8,128)} %fusion.12, f32[768,1536]{1,0:T(8,128)} %fusion.8, bf16[768,1536]{1,0:T(8,128)(2,1)} %all-gather.21.cloned.1.call-done, bf16[1536,6144]{1,0:T(8,128)(2,1)} %param.10), kind=kOutput, calls=%fused_computation.14 | convolution fusion | flops 3628597248 | bytes 23592960 | tf_op jit(solution)/shard_map/dot_general | solution.py:17
  461.8 10.4 %all-reduce.1 = (f32[192]{0:T(256)S(1)}, f32[192]{0:T(256)S(1)}) all-reduce(f32[192]{0:T(256)S(1)} %get-tuple-element.9, f32[192]{0:T(256)S(1)} %get-tuple-element.8), channel_id=1, replica_groups=mesh['dp'=2,'row'=4,'col'=4] {'row'}, use_global_device_ids=true, to_apply=%region_3.0 | all-reduce | flops 384 | bytes 3072 | tf_op jit(solution)/shard_map/psum | solution.py:42
  472.3 26.1 %all-gather.31.cloned.1.call-done = bf16[768,1536]{1,0:T(8,128)(2,1)} async-done(((bf16[192,1536]{1,0:T(8,128)(2,1)}), bf16[768,1536]{1,0:T(8,128)(2,1)}) %all-gather.31.cloned.1.call-update) | async-done | bytes 2359312 | tf_op jit(solution)/shard_map/all_gather | solution.py:85
  505.0 43.8 %all-gather.29.cloned.1.call-done = bf16[768,1536]{1,0:T(8,128)(2,1)} async-done(((bf16[192,1536]{1,0:T(8,128)(2,1)}), bf16[768,1536]{1,0:T(8,128)(2,1)}) %all-gather.29.cloned.1.call-update) | async-done | bytes 2359312 | tf_op jit(solution)/shard_map/all_gather | solution.py:85
  555.3 43.6 %all-gather.27.cloned.1.call-done = bf16[768,1536]{1,0:T(8,128)(2,1)} async-done(((bf16[192,1536]{1,0:T(8,128)(2,1)}), bf16[768,1536]{1,0:T(8,128)(2,1)}) %all-gather.27.cloned.1.call-update) | async-done | bytes 2359312 | tf_op jit(solution)/shard_map/all_gather | solution.py:85
  605.6 44.3 %all-gather.25.cloned.1.call-done = bf16[768,1536]{1,0:T(8,128)(2,1)} async-done(((bf16[192,1536]{1,0:T(8,128)(2,1)}), bf16[768,1536]{1,0:T(8,128)(2,1)}) %all-gather.25.cloned.1.call-update) | async-done | bytes 2359312 | tf_op jit(solution)/shard_map/all_gather | solution.py:85
  656.4 27.4 %reduce-scatter.14.cloned.1.call-done = bf16[192,1536]{1,0:T(8,128)(2,1)} async-done(((bf16[768,1536]{1,0:T(8,128)(2,1)}), bf16[192,1536]{1,0:T(8,128)(2,1)}) %reduce-scatter.14.cloned.1.call-update) | async-done | bytes 589840 | tf_op jit(solution)/shard_map/reduce_scatter | solution.py:97
  692.3 16.4 %collective-permute-done.8 = f32[6144]{0:T(1024)S(1)} collective-permute-done((f32[6144]{0:T(1024)S(1)}, f32[6144]{0:T(1024)S(1)}, u32[]{:S(2)}, u32[]{:S(2)}) %collective-permute-start.8) | collective-permute-done | bytes 24608 | tf_op jit(solution)/shard_map/ppermute | solution.py:94
  760.3 138.3 %all-gather.1 = f32[8,1,1536]{2,1,0:T(1,128)S(1)} all-gather(f32[1,1,1536]{2,1,0:T(1,128)S(1)} %reshape.18), channel_id=2, replica_groups=mesh['dp'=2,'row'=4,'col'=4] {'dp','col'}, dimensions={0}, use_global_device_ids=true | all-gather | bytes 55296 | tf_op jit(solution)/shard_map/all_gather | solution.py:106
  899.3 9.9 %all-reduce = (f32[192]{0:T(256)S(1)}, f32[192]{0:T(256)S(1)}) all-reduce(f32[192]{0:T(256)S(1)} %get-tuple-element.6, f32[192]{0:T(256)S(1)} %get-tuple-element.7), channel_id=1, replica_groups=mesh['dp'=2,'row'=4,'col'=4] {'row'}, use_global_device_ids=true, to_apply=%region_12.0 | all-reduce | flops 384 | bytes 3072 | tf_op jit(solution)/shard_map/psum | solution.py:101
  928.1 36.8 %collective-permute-done.3 = bf16[768,1536]{1,0:T(8,128)(2,1)S(1)} collective-permute-done((bf16[768,1536]{1,0:T(8,128)(2,1)S(1)}, bf16[768,1536]{1,0:T(8,128)(2,1)S(1)}, u32[]{:S(2)}, u32[]{:S(2)}) %collective-permute-start.3) | collective-permute-done | bytes 2359328 | tf_op jit(solution)/shard_map/ppermute | solution.py:63
  (135 shorter events, 151.9 us)
Async XLA Ops:
  7.2 29.2 %all-gather.13.cloned.1.call-start = ((), (), s32[]{:S(2)}) async-start(), calls=%async_computation.5 | async-start | bytes 2949120 | tf_op jit(solution)/shard_map/all_gather | solution.py:40
  7.9 84.6 %reduce-scatter.10.cloned.1.call-start = ((), (), s32[]{:S(2)}) async-start(), calls=%async_computation.10 | async-start | bytes 2949120 | tf_op jit(solution)/shard_map/reduce_scatter | solution.py:79
  44.7 97.8 %reduce-scatter.12.cloned.1.call-start = ((), (), s32[]{:S(2)}) async-start(), calls=%async_computation.12 | async-start | bytes 2949120 | tf_op jit(solution)/shard_map/reduce_scatter | solution.py:79
  53.7 138.1 %reduce-scatter.6.cloned.1.call-start = ((), (), s32[]{:S(2)}) async-start(), calls=%async_computation.6 | async-start | bytes 2949120 | tf_op jit(solution)/shard_map/reduce_scatter | solution.py:79
  61.2 179.8 %reduce-scatter.8.cloned.1.call-start = ((), (), s32[]{:S(2)}) async-start(), calls=%async_computation.8 | async-start | bytes 2949120 | tf_op jit(solution)/shard_map/reduce_scatter | solution.py:79
  68.7 227.6 %all-gather.15.cloned.1.call-start = ((), (), s32[]{:S(2)}) async-start(), calls=%async_computation.7 | async-start | bytes 2949120 | tf_op jit(solution)/shard_map/all_gather | solution.py:87
  246.8 100.5 %all-gather.19.cloned.1.call-start = ((), (), s32[]{:S(2)}) async-start(), calls=%async_computation.11 | async-start | bytes 2949120 | tf_op jit(solution)/shard_map/all_gather | solution.py:87
  247.5 150.0 %all-gather.17.cloned.1.call-start = ((), (), s32[]{:S(2)}) async-start(), calls=%async_computation.9 | async-start | bytes 2949120 | tf_op jit(solution)/shard_map/all_gather | solution.py:87
  248.3 199.7 %all-gather.21.cloned.1.call-start = ((), (), s32[]{:S(2)}) async-start(), calls=%async_computation.13 | async-start | bytes 2949120 | tf_op jit(solution)/shard_map/all_gather | solution.py:87
  249.0 249.4 %all-gather.31.cloned.1.call-start = ((), (), s32[]{:S(2)}) async-start(), calls=%async_computation.19 | async-start | bytes 2949120 | tf_op jit(solution)/shard_map/all_gather | solution.py:85
  249.6 299.1 %all-gather.29.cloned.1.call-start = ((), (), s32[]{:S(2)}) async-start(), calls=%async_computation.18 | async-start | bytes 2949120 | tf_op jit(solution)/shard_map/all_gather | solution.py:85
  250.4 348.6 %all-gather.27.cloned.1.call-start = ((), (), s32[]{:S(2)}) async-start(), calls=%async_computation.17 | async-start | bytes 2949120 | tf_op jit(solution)/shard_map/all_gather | solution.py:85
  250.9 398.9 %all-gather.25.cloned.1.call-start = ((), (), s32[]{:S(2)}) async-start(), calls=%async_computation.16 | async-start | bytes 2949120 | tf_op jit(solution)/shard_map/all_gather | solution.py:85
  251.7 432.2 %reduce-scatter.14.cloned.1.call-start = ((), (), s32[]{:S(2)}) async-start(), calls=%async_computation.14 | async-start | bytes 2949120 | tf_op jit(solution)/shard_map/reduce_scatter | solution.py:97
  460.6 274.4 %all-gather.23.cloned.1.call-start = ((), (), s32[]{:S(2)}) async-start(), calls=%async_computation.15 | async-start | bytes 2949120 | tf_op jit(solution)/shard_map/all_gather | solution.py:47
  503.5 205.9 %collective-permute-start.7 = (bf16[1536,768]{1,0:T(8,128)(2,1)}, bf16[1536,768]{1,0:T(8,128)(2,1)}, u32[]{:S(2)}, u32[]{:S(2)}) collective-permute-start(bf16[1536,768]{1,0:T(8,128)(2,1)} %convolution_convert_fusion), channel_id=1, source_target_pairs={{0,16},{16,0},{1,17},{17,1},{2,18},{18,2},{3,19},{19,3},{4,20},{20... | collective-permute-start | bytes 7077896 | tf_op jit(solution)/shard_map/ppermute | solution.py:72
  553.9 163.1 %collective-permute-start.6 = (bf16[1536,768]{1,0:T(8,128)(2,1)}, bf16[1536,768]{1,0:T(8,128)(2,1)}, u32[]{:S(2)}, u32[]{:S(2)}) collective-permute-start(bf16[1536,768]{1,0:T(8,128)(2,1)} %convolution_convert_fusion.1), channel_id=1, source_target_pairs={{0,16},{16,0},{1,17},{17,1},{2,18},{18,2},{3,19},{19,3},{4,20},{20... | collective-permute-start | bytes 7077896 | tf_op jit(solution)/shard_map/ppermute | solution.py:72
  604.1 118.9 %collective-permute-start.5 = (bf16[1536,768]{1,0:T(8,128)(2,1)}, bf16[1536,768]{1,0:T(8,128)(2,1)}, u32[]{:S(2)}, u32[]{:S(2)}) collective-permute-start(bf16[1536,768]{1,0:T(8,128)(2,1)} %convolution_convert_fusion.2), channel_id=1, source_target_pairs={{0,16},{16,0},{1,17},{17,1},{2,18},{18,2},{3,19},{19,3},{4,20},{20... | collective-permute-start | bytes 7077896 | tf_op jit(solution)/shard_map/ppermute | solution.py:72
  655.0 74.1 %collective-permute-start.4 = (bf16[1536,768]{1,0:T(8,128)(2,1)}, bf16[1536,768]{1,0:T(8,128)(2,1)}, u32[]{:S(2)}, u32[]{:S(2)}) collective-permute-start(bf16[1536,768]{1,0:T(8,128)(2,1)} %convolution_convert_fusion.3), channel_id=1, source_target_pairs={{0,16},{16,0},{1,17},{17,1},{2,18},{18,2},{3,19},{19,3},{4,20},{20... | collective-permute-start | bytes 7077896 | tf_op jit(solution)/shard_map/ppermute | solution.py:72
  690.8 18.0 %collective-permute-start.8 = (f32[6144]{0:T(1024)S(1)}, f32[6144]{0:T(1024)S(1)}, u32[]{:S(2)}, u32[]{:S(2)}) collective-permute-start(f32[6144]{0:T(1024)S(1)} %pad_maximum_fusion.2), channel_id=1, source_target_pairs={{0,16},{16,0},{1,17},{17,1},{2,18},{18,2},{3,19},{19,3},{4,20},{20... | collective-permute-start | bytes 73736 | tf_op jit(solution)/shard_map/ppermute | solution.py:94
  740.6 175.8 %collective-permute-start = (bf16[768,1536]{1,0:T(8,128)(2,1)}, bf16[768,1536]{1,0:T(8,128)(2,1)}, u32[]{:S(2)}, u32[]{:S(2)}) collective-permute-start(bf16[768,1536]{1,0:T(8,128)(2,1)} %convolution_convert_fusion.7), channel_id=1, source_target_pairs={{0,16},{16,0},{1,17},{17,1},{2,18},{18,2},{3,19},{19,3},{4,20},{20... | collective-permute-start | bytes 7077896 | tf_op jit(solution)/shard_map/ppermute | solution.py:63
  747.7 172.6 %collective-permute-start.1 = (bf16[768,1536]{1,0:T(8,128)(2,1)}, bf16[768,1536]{1,0:T(8,128)(2,1)}, u32[]{:S(2)}, u32[]{:S(2)}) collective-permute-start(bf16[768,1536]{1,0:T(8,128)(2,1)} %convolution_convert_fusion.6), channel_id=1, source_target_pairs={{0,16},{16,0},{1,17},{17,1},{2,18},{18,2},{3,19},{19,3},{4,20},{20... | collective-permute-start | bytes 7077896 | tf_op jit(solution)/shard_map/ppermute | solution.py:63
  758.7 165.4 %collective-permute-start.2 = (bf16[768,1536]{1,0:T(8,128)(2,1)}, bf16[768,1536]{1,0:T(8,128)(2,1)}, u32[]{:S(2)}, u32[]{:S(2)}) collective-permute-start(bf16[768,1536]{1,0:T(8,128)(2,1)} %convolution_convert_fusion.5), channel_id=1, source_target_pairs={{0,16},{16,0},{1,17},{17,1},{2,18},{18,2},{3,19},{19,3},{4,20},{20... | collective-permute-start | bytes 7077896 | tf_op jit(solution)/shard_map/ppermute | solution.py:63
  913.4 51.5 %collective-permute-start.3 = (bf16[768,1536]{1,0:T(8,128)(2,1)S(1)}, bf16[768,1536]{1,0:T(8,128)(2,1)S(1)}, u32[]{:S(2)}, u32[]{:S(2)}) collective-permute-start(bf16[768,1536]{1,0:T(8,128)(2,1)S(1)} %convolution_convert_fusion.4), channel_id=1, source_target_pairs={{0,16},{16,0},{1,17},{17,1},{2,18},{18,2},{3,19},{19,3},{4,20},{20... | collective-permute-start | bytes 7077896 | tf_op jit(solution)/shard_map/ppermute | solution.py:63
  (25 other events, 466.4 us)
Sparse Core Ops, SparseCore 0:
  9.5 26.7 all-gather.12
  44.8 47.6 reduce-scatter.9
  95.4 47.0 reduce-scatter.11
  144.7 47.1 reduce-scatter.5
  194.0 47.0 reduce-scatter.7
  246.9 49.3 all-gather.14
  298.5 48.7 all-gather.18
  348.8 48.7 all-gather.16
  399.2 48.7 all-gather.20
  449.4 48.9 all-gather.30
  500.0 48.7 all-gather.28
  550.2 48.7 all-gather.26
  601.1 48.7 all-gather.24
  652.3 31.5 reduce-scatter.13
  686.6 24.0 all-gather.22
